TPU v7x, 256 devices: a whole 4x4x8 slice. The times are simulated.
256 devices in a mesh: dp: 8 (over x, core), expert: 32 (over z, y).
Axes of the slice: x: 4, y: 4, z: 8, core: 2. Of those that a mesh axis runs over, the one named last changes fastest.
Arguments:
- tokens: bfloat16 [2048, 3584], P(('dp', 'expert')), may hold values from -6 to 6
- cotangent: bfloat16 [2048, 3584], P(('dp', 'expert')), may hold values from -6 to 6
- routes: int32 [2048, 8], P(('dp', 'expert')), may hold values from 0 to 31, all different within a row; in each aligned block of 8 rows (0 to 7, 8 to 15, ...) at most 3 rows name the same one
- gates: bfloat16 [2048, 8], P(('dp', 'expert')), may hold values from 0.049804688 to 1
- w_gate: bfloat16 [32, 3584, 2048], P('expert', None, 'dp'), may hold values from -0.09375 to 0.09375
- w_up: bfloat16 [32, 3584, 2048], P('expert', None, 'dp'), may hold values from -0.09375 to 0.09375
- w_down: bfloat16 [32, 2048, 3584], P('expert', 'dp'), may hold values from -0.125 to 0.125
Outputs:
- grad_tokens: bfloat16 [2048, 3584], P(('dp', 'expert'))
- grad_gate: bfloat16 [32, 3584, 2048], P('expert', None, 'dp')
- grad_up: bfloat16 [32, 3584, 2048], P('expert', None, 'dp')
- grad_down: bfloat16 [32, 2048, 3584], P('expert', 'dp')
Inputs may be any that keep to these rules, and one draw needn't show every extreme that they name: `routes`: each row names 8 different experts; among the rows of one device no expert is named more than 3 times, a bound that some block reaches.
All inputs are finite; a program needn't handle non-finite values.
Results may differ from a plain program's by a relative error of at most 0.01.
Values may be sent and summed in bfloat16 or wider, within the bound.
No kernel may reach another device: no remote copies, remote signals or barrier semaphores. Data moves between devices by JAX's collectives and lax.ppermute only.
A program may use at most 128 MiB of HBM per device.

v0:
```python
import math
import jax
import jax.numpy as jnp
from jax import lax
from jax.sharding import PartitionSpec as P


def in_one_piece(arrays, axis, split_dim, concat_dim, along):
    widths = [math.prod(a.shape[along:]) for a in arrays]
    both = jnp.concatenate(
        [a.reshape(*a.shape[:along], w) for a, w in zip(arrays, widths)], axis=along
    )
    out = lax.all_to_all(both, axis, split_axis=split_dim, concat_axis=concat_dim, tiled=True)
    parts = jnp.split(out, [sum(widths[:k]) for k in range(1, len(widths))], axis=along)
    return tuple((b.reshape(*out.shape[:along], *a.shape[along:]) for a, b in zip(arrays, parts)))


def slot_index(flat_ids, expert_count):
    onehot = (flat_ids[..., None] == jnp.arange(expert_count, dtype=jnp.int32)).astype(jnp.int32)
    return jnp.sum((jnp.cumsum(onehot, axis=-2) - onehot) * onehot, axis=-1)


def expert_terms(rows_x, rows_dy, gate_rows, gate_mat, up_mat, down_mat):
    gate_pre = jnp.dot(rows_x, gate_mat, preferred_element_type=jnp.float32)
    up_pre = jnp.dot(rows_x, up_mat, preferred_element_type=jnp.float32)
    sigmoid_g = jax.nn.sigmoid(gate_pre)
    activated = gate_pre * sigmoid_g
    gate_scale = gate_rows.astype(jnp.float32)[:, None]
    hidden = (gate_scale * activated * up_pre).astype(jnp.bfloat16)
    returned = gate_scale * jnp.dot(rows_dy, down_mat.T, preferred_element_type=jnp.float32)
    d_gate = (returned * up_pre * sigmoid_g * (1.0 + gate_pre * (1.0 - sigmoid_g))).astype(
        jnp.bfloat16
    )
    d_up = (returned * activated).astype(jnp.bfloat16)
    grad_gate = jnp.dot(rows_x.T, d_gate, preferred_element_type=jnp.float32)
    grad_up = jnp.dot(rows_x.T, d_up, preferred_element_type=jnp.float32)
    grad_down = jnp.dot(hidden.T, rows_dy, preferred_element_type=jnp.float32)
    return (d_gate, d_up, grad_gate, grad_up, grad_down)


def per_device(tokens, cotangent, routes, gates, w_gate, w_up, w_down):
    tok_rows, features = tokens.shape
    top_k = routes.shape[1]
    expert_count = lax.axis_size("expert")
    capacity = min(tok_rows, (3 * tok_rows * top_k + 2 * expert_count - 1) // (2 * expert_count))
    gate_mat = w_gate[0]
    up_mat = w_up[0]
    down_mat = w_down[0]
    flat_ids = routes.reshape(-1)
    position = flat_ids * capacity + slot_index(flat_ids, expert_count)
    token_of = jnp.arange(tok_rows * top_k, dtype=jnp.int32) // top_k
    slots_all = expert_count * capacity
    send_x = jnp.zeros((slots_all, features), jnp.bfloat16).at[position].set(tokens[token_of])
    send_dy = jnp.zeros((slots_all, features), jnp.bfloat16).at[position].set(cotangent[token_of])
    send_gate = jnp.zeros((slots_all,), jnp.bfloat16).at[position].set(gates.reshape(-1))
    received = in_one_piece(
        (
            send_x.reshape(expert_count, capacity, features),
            send_dy.reshape(expert_count, capacity, features),
            send_gate.reshape(expert_count, capacity),
        ),
        "expert",
        0,
        0,
        2,
    )
    gathered = (
        lax.all_gather(received[0], "dp", axis=0, tiled=True),
        lax.all_gather(received[1], "dp", axis=0, tiled=True),
        lax.all_gather(received[2], "dp", axis=0, tiled=True),
    )
    rows_x = gathered[0].reshape(-1, features)
    rows_dy = gathered[1].reshape(-1, features)
    d_gate, d_up, grad_gate, grad_up, grad_down = expert_terms(
        rows_x, rows_dy, gathered[2].reshape(-1), gate_mat, up_mat, down_mat
    )
    own_rows = lax.psum_scatter(
        (
            jnp.dot(d_gate, gate_mat.T, preferred_element_type=jnp.float32)
            + jnp.dot(d_up, up_mat.T, preferred_element_type=jnp.float32)
        ).astype(jnp.bfloat16),
        "dp",
        scatter_dimension=0,
        tiled=True,
    ).astype(jnp.float32)
    returned = lax.all_to_all(
        own_rows.reshape(expert_count, capacity, features).astype(jnp.bfloat16),
        "expert",
        split_axis=0,
        concat_axis=0,
        tiled=True,
    ).astype(jnp.float32)
    selected = returned.reshape(slots_all, features)[position]
    grad_x = selected.reshape(tok_rows, top_k, features).sum(axis=1)
    return (
        grad_x.astype(jnp.bfloat16),
        grad_gate.astype(jnp.bfloat16)[None],
        grad_up.astype(jnp.bfloat16)[None],
        grad_down.astype(jnp.bfloat16)[None],
    )


def solution(mesh):
    return jax.shard_map(
        per_device,
        mesh=mesh,
        in_specs=(
            P(("dp", "expert"), None),
            P(("dp", "expert"), None),
            P(("dp", "expert"), None),
            P(("dp", "expert"), None),
            P("expert", None, "dp"),
            P("expert", None, "dp"),
            P("expert", "dp", None),
        ),
        out_specs=(
            P(("dp", "expert"), None),
            P("expert", None, "dp"),
            P("expert", None, "dp"),
            P("expert", "dp", None),
        ),
        check_vma=False,
    )
```

profile of v0, /device:TPU:15, one launch (start us, length us, event | category | flops | bytes accessed | tf_op | source)
XLA Modules:
  0.0 286.5 jit_solution(9832261786138127804)
XLA Ops:
  7.2 0.0 copy-start
  7.2 0.0 copy-start.6
  7.2 0.0 all-gather.6.cloned.1.call-start
  7.2 0.9 eq.15
  8.1 0.7 broadcast_multiply_fusion
  8.8 0.1 fusion.24
  8.9 0.1 reduce_window_sum.11
  9.0 0.2 select_reduce_fusion
  9.2 0.1 mul.58
  9.3 4.0 %scatter_custom_fusion = bf16[96,3584]{1,0:T(8,128)(2,1)S(1)} fusion(s32[64]{0:T(128)S(1)} %fusion.26, bf16[8,3584]{1,0:T(8,128)(2,1)} %param.7, s32[1024]{0:T(1024)S(1)} %pad_clamp_fusion.1, bf16[]{:T(256)} %constant.26.clone.1), kind=kCustom, calls=%fused_computation.32 | custom fusion | bytes 688640 | tf_op jit(solution)/shard_map/scatter | solution.py:53
  13.3 0.4 reshape.118
  13.7 4.0 %scatter_custom_fusion.1 = bf16[96,3584]{1,0:T(8,128)(2,1)S(1)} fusion(s32[64]{0:T(128)S(1)} %fusion.26, bf16[8,3584]{1,0:T(8,128)(2,1)} %param.8, s32[1024]{0:T(1024)S(1)} %pad_clamp_fusion.1, bf16[]{:T(256)} %constant.26.clone.1), kind=kCustom, calls=%fused_computation.30 | custom fusion | bytes 688640 | tf_op jit(solution)/shard_map/scatter | solution.py:54
  17.7 1.2 reshape.119
  18.8 0.0 copy-done.6
  18.8 0.1 reshape.174
  18.9 1.0 scatter_custom_fusion.2
  19.9 0.2 reshape_reshape.4
  20.1 1.9 pad_maximum_fusion
  22.0 55.3 %all_to_all.10 = bf16[32,3,7169]{2,1,0:T(4,128)(2,1)S(1)} all-to-all(bf16[32,3,7169]{2,1,0:T(4,128)(2,1)S(1)} %pad_maximum_fusion), channel_id=1, replica_groups=mesh['dp'=8,'expert'=32] {'expert'}, dimensions={0} | all-to-all | bytes 2752896 | tf_op jit(solution)/shard_map/all_to_all | solution.py:13
  77.3 1.3 copy-done.1
  78.6 0.6 fusion.30
  79.3 0.0 slice-start
  79.3 1.0 copy.17
  80.3 0.0 all-gather.6.cloned.1.call-update
  80.3 0.0 all-gather.4.cloned.1.call-start
  80.3 1.0 copy.15
  81.3 0.0 all-gather.4.cloned.1.call-update
  81.4 0.0 reduce-scatter.2.cloned.1.call-start
  81.4 0.0 slice-done
  81.4 0.3 copy.14
  81.7 15.5 %all-gather = bf16[256,3,1]{1,2,0:T(2,128)(2,1)S(1)} all-gather(bf16[32,3,1]{1,2,0:T(2,128)(2,1)S(1)} %copy.14), channel_id=2, replica_groups=mesh['dp'=8,'expert'=32] {'dp'}, dimensions={0}, use_global_device_ids=true | all-gather | bytes 1728 | tf_op jit(solution)/shard_map/all_gather | solution.py:70
  97.2 0.4 convert_reduce_fusion
  97.6 0.2 reshape.127
  97.8 19.9 %all-gather.6.cloned.1.call-done = bf16[256,3,3584]{2,0,1:T(8,128)(2,1)} async-done(((bf16[32,3,3584]{2,0,1:T(8,128)(2,1)}), bf16[256,3,3584]{2,0,1:T(8,128)(2,1)}) %all-gather.6.cloned.1.call-update) | async-done | bytes 5505040 | tf_op jit(solution)/shard_map/all_gather | solution.py:68
  117.7 10.2 %copy.18 = bf16[256,3,3584]{2,1,0:T(4,128)(2,1)} copy(bf16[256,3,3584]{2,0,1:T(8,128)(2,1)} %all-gather.6.cloned.1.call-done) | data formatting | bytes 11010048 | tf_op jit(solution)/shard_map/all_gather | solution.py:68
  127.9 13.1 %reshape.123 = bf16[768,3584]{1,0:T(8,128)(2,1)} reshape(bf16[256,3,3584]{2,1,0:T(4,128)(2,1)} %copy.18) | data formatting | bytes 11010048 | tf_op jit(solution)/shard_map/reshape | solution.py:72
  141.0 0.0 copy-done
  141.0 4.4 %fusion.5 = f32[768,256]{1,0:T(8,128)S(1)} fusion(bf16[768,3584]{1,0:T(8,128)(2,1)} %reshape.123, bf16[1,3584,256]{2,1,0:T(8,128)(2,1)S(1)} %copy-done), kind=kOutput, calls=%fused_computation.16 | convolution fusion | flops 1409286144 | bytes 8126464 | tf_op jit(solution)/shard_map/dot_general | solution.py:24
  145.4 0.6 copy-done.3
  146.0 2.5 fusion.8
  148.4 11.7 %all-gather.4.cloned.1.call-done = bf16[256,3,3584]{2,0,1:T(8,128)(2,1)} async-done(((bf16[32,3,3584]{2,0,1:T(8,128)(2,1)}), bf16[256,3,3584]{2,0,1:T(8,128)(2,1)}) %all-gather.4.cloned.1.call-update) | async-done | bytes 5505040 | tf_op jit(solution)/shard_map/all_gather | solution.py:69
  160.1 10.2 %copy.16 = bf16[256,3,3584]{2,1,0:T(4,128)(2,1)} copy(bf16[256,3,3584]{2,0,1:T(8,128)(2,1)} %all-gather.4.cloned.1.call-done) | data formatting | bytes 11010048 | tf_op jit(solution)/shard_map/all_gather | solution.py:69
  170.4 13.0 %reshape.122 = bf16[768,3584]{1,0:T(8,128)(2,1)} reshape(bf16[256,3,3584]{2,1,0:T(4,128)(2,1)} %copy.16) | data formatting | bytes 11010048 | tf_op jit(solution)/shard_map/reshape | solution.py:73
  183.4 5.0 %multiply_convert_fusion.1 = (bf16[768,256]{1,0:T(8,128)(2,1)S(1)}, bf16[768,256]{1,0:T(8,128)(2,1)S(1)}) fusion(f32[768,256]{1,0:T(8,128)S(1)} %fusion.5, f32[768,256]{1,0:T(8,128)} %fusion.8, bf16[768,3584]{1,0:T(8,128)(2,1)} %reshape.122, bf16[1,256,3584]{2,1,0:T(8,128)(2,1)} %param.13, f32[768]{0:T(1024)S(1)} %reshape.127), kind=kOutput, calls=%fused_computation.26 | convolution fusion | flops 1412038656 | bytes 9702400 | tf_op jit(solution)/shard_map/dot_general | solution.py:30
  188.4 0.0 copy-start.5
  188.4 0.0 copy-start.4
  188.4 1.6 fusion.3
  190.1 4.0 %add_convert_fusion = bf16[768,3584]{1,0:T(8,128)(2,1)} fusion(f32[768,3584]{1,0:T(8,128)S(1)} %fusion.3, bf16[768,256]{1,0:T(8,128)(2,1)S(1)} %get-tuple-element.6, bf16[1,3584,256]{2,1,0:T(8,128)(2,1)S(1)} %copy-done.4), kind=kOutput, calls=%fused_computation.6 | convolution fusion | flops 1414791168 | bytes 18743296 | tf_op jit(solution)/shard_map/dot_general | solution.py:80
  194.1 0.0 reduce-scatter.2.cloned.1.call-update
  194.2 43.8 %reduce-scatter.2.cloned.1.call-done = bf16[96,3584]{1,0:T(8,128)(2,1)} async-done(((bf16[768,3584]{1,0:T(8,128)(2,1)}), bf16[96,3584]{1,0:T(8,128)(2,1)}) %reduce-scatter.2.cloned.1.call-update) | async-done | bytes 688144 | tf_op jit(solution)/shard_map/reduce_scatter | solution.py:77
  238.0 2.1 convert_element_type.49
  240.1 9.7 %all-to-all-start.1 = ((bf16[32,3,3584]{2,1,0:T(4,128)(2,1)}), bf16[32,3,3584]{2,1,0:T(4,128)(2,1)}, u32[]{:S(2)}, u32[]{:S(2)}) async-start(bf16[32,3,3584]{2,1,0:T(4,128)(2,1)} %convert_element_type.49), calls=%async_computation.2 | async-start | bytes 1835008 | tf_op jit(solution)/shard_map/all_to_all | solution.py:86
  249.8 0.0 slice-start.2
  249.8 0.0 slice-start.3
  249.9 5.6 %fusion.1 = bf16[1,3584,256]{2,1,0:T(8,128)(2,1)} fusion(bf16[768,3584]{1,0:T(8,128)(2,1)} %reshape.123, bf16[768,256]{1,0:T(8,128)(2,1)} %copy-done.5), kind=kOutput, calls=%fused_computation.11 | convolution fusion | flops 1410203648 | bytes 7733248 | tf_op jit(solution)/shard_map/dot_general | solution.py:36
  255.5 0.0 copy-start.9
  255.5 2.9 %fusion = bf16[1,3584,256]{2,1,0:T(8,128)(2,1)} fusion(bf16[768,3584]{1,0:T(8,128)(2,1)S(1)} %bitcast.44, bf16[768,256]{1,0:T(8,128)(2,1)S(1)} %get-tuple-element.7), kind=kOutput, calls=%fused_computation.10 | convolution fusion | flops 1410203648 | bytes 7733248 | tf_op jit(solution)/shard_map/dot_general | solution.py:35
  258.4 0.0 slice-done.3
  258.4 0.0 copy-done.8
  258.4 3.0 %fusion.2 = bf16[1,256,3584]{2,1,0:T(8,128)(2,1)} fusion(bf16[768,3584]{1,0:T(8,128)(2,1)S(1)} %bitcast.46, f32[768,256]{1,0:T(8,128)S(1)} %copy-done.9, f32[768]{0:T(1024)S(1)} %reshape.127, f32[768,256]{1,0:T(8,128)S(1)} %copy-done.8), kind=kOutput, calls=%fused_computation.12 | convolution fusion | flops 1411579904 | bytes 8915968 | tf_op jit(solution)/shard_map/dot_general | solution.py:37
  261.5 13.1 %all-to-all-done.1 = bf16[32,3,3584]{2,1,0:T(4,128)(2,1)} async-done(((bf16[32,3,3584]{2,1,0:T(4,128)(2,1)}), bf16[32,3,3584]{2,1,0:T(4,128)(2,1)}, u32[]{:S(2)}, u32[]{:S(2)}) %all-to-all-start.1) | async-done | bytes 688160 | tf_op jit(solution)/shard_map/all_to_all | solution.py:86
  274.6 1.6 reshape.129
  276.1 1.8 gather_fusion
  277.9 2.0 bitcast_reduce_fusion
  (21 shorter events, 0.1 us)
Async XLA Ops:
  7.2 133.8 %copy-start = (bf16[1,3584,256]{2,1,0:T(8,128)(2,1)S(1)}, bf16[1,3584,256]{2,1,0:T(8,128)(2,1)}, u32[]{:S(2)}) copy-start(bf16[1,3584,256]{2,1,0:T(8,128)(2,1)} %param.11) | copy-start | bytes 5505028
  7.2 11.7 %copy-start.6 = (bf16[8,8]{1,0:T(8,128)(2,1)S(1)}, bf16[8,8]{1,0:T(8,128)(2,1)}, u32[]{:S(2)}) copy-start(bf16[8,8]{1,0:T(8,128)(2,1)} %param.10) | copy-start | bytes 388
  7.2 110.5 %all-gather.6.cloned.1.call-start = ((), (), s32[]{:S(2)}) async-start(), calls=%async_computation.4 | async-start | bytes 6193152 | tf_op jit(solution)/shard_map/all_gather | solution.py:68
  77.3 1.3 copy-start.1
  79.3 2.2 slice-start
  80.3 79.9 %all-gather.4.cloned.1.call-start = ((), (), s32[]{:S(2)}) async-start(), calls=%async_computation.3 | async-start | bytes 6193152 | tf_op jit(solution)/shard_map/all_gather | solution.py:69
  81.4 156.6 %reduce-scatter.2.cloned.1.call-start = ((), (), s32[]{:S(2)}) async-start(), calls=%async_computation.5 | async-start | bytes 6193152 | tf_op jit(solution)/shard_map/reduce_scatter | solution.py:77
  141.0 4.4 %copy-start.2 = (bf16[768,3584]{1,0:T(8,128)(2,1)S(1)}, bf16[768,3584]{1,0:T(8,128)(2,1)}, u32[]{:S(2)}) copy-start(bf16[768,3584]{1,0:T(8,128)(2,1)} %reshape.123) | copy-start | bytes 16515076
  141.0 5.0 %copy-start.3 = (bf16[1,3584,256]{2,1,0:T(8,128)(2,1)S(1)}, bf16[1,3584,256]{2,1,0:T(8,128)(2,1)}, u32[]{:S(2)}) copy-start(bf16[1,3584,256]{2,1,0:T(8,128)(2,1)} %param.12) | copy-start | bytes 5505028
  146.0 37.4 %copy-start.7 = (f32[768,256]{1,0:T(8,128)}, f32[768,256]{1,0:T(8,128)S(1)}, u32[]{:S(2)}) copy-start(f32[768,256]{1,0:T(8,128)S(1)} %fusion.5) | copy-start | bytes 2359300
  188.4 1.7 copy-start.5
  188.4 1.7 copy-start.4
  240.1 15.4 %slice-start.1 = ((s8[5505024]{0:T(1024)(128)(4,1)}), s8[1310720]{0:T(1024)(128)(4,1)S(1)}, s32[]{:S(2)}) async-start(s8[5505024]{0:T(1024)(128)(4,1)} %bitcast.43), calls=%async_computation.7 | async-start | bytes 2621440
  240.1 34.5 %all-to-all-start.1 = ((bf16[32,3,3584]{2,1,0:T(4,128)(2,1)}), bf16[32,3,3584]{2,1,0:T(4,128)(2,1)}, u32[]{:S(2)}, u32[]{:S(2)}) async-start(bf16[32,3,3584]{2,1,0:T(4,128)(2,1)} %convert_element_type.49), calls=%async_computation.2 | async-start | bytes 1835008 | tf_op jit(solution)/shard_map/all_to_all | solution.py:86
  249.8 5.7 %slice-start.2 = ((s8[5505024]{0:T(1024)(128)(4,1)}), s8[4194304]{0:T(1024)(128)(4,1)S(1)}, s32[]{:S(2)}) async-start(s8[5505024]{0:T(1024)(128)(4,1)} %bitcast.43), calls=%async_computation.8 | async-start | bytes 8388608
  249.8 8.6 %slice-start.3 = ((s8[5505024]{0:T(1024)(128)(4,1)}), s8[4194304]{0:T(1024)(128)(4,1)S(1)}, s32[]{:S(2)}) async-start(s8[5505024]{0:T(1024)(128)(4,1)} %bitcast.45), calls=%async_computation.9 | async-start | bytes 8388608
  255.5 2.9 %slice-start.4 = ((s8[5505024]{0:T(1024)(128)(4,1)}), s8[1310720]{0:T(1024)(128)(4,1)S(1)}, s32[]{:S(2)}) async-start(s8[5505024]{0:T(1024)(128)(4,1)} %bitcast.45), calls=%async_computation.10 | async-start | bytes 2621440
  255.5 2.9 %copy-start.8 = (f32[768,256]{1,0:T(8,128)S(1)}, f32[768,256]{1,0:T(8,128)}, u32[]{:S(2)}) copy-start(f32[768,256]{1,0:T(8,128)} %copy-done.7) | copy-start | bytes 2359300
  255.5 2.9 %copy-start.9 = (f32[768,256]{1,0:T(8,128)S(1)}, f32[768,256]{1,0:T(8,128)}, u32[]{:S(2)}) copy-start(f32[768,256]{1,0:T(8,128)} %fusion.8) | copy-start | bytes 2359300
Sparse Core Ops, SparseCore 0:
  80.4 37.1 all-gather.5
  120.1 40.0 all-gather.3
  194.3 43.6 reduce-scatter.1
where the time goes:
time: 288 us; the launch traced here: 286 us
  waiting for transfers between devices  88.5 us (31%)
  blocking collectives  70.8 us (25%)
  local copies, waits for them, and re-layouts  68.8 us (24%)
  matrix products  29.1 us (10%)
  between operations  14 us (5%)
  starting transfers between devices  9.84 us (3%)
  other arithmetic  5.39 us (2%)
    all_to_all x1, blocking collectives, in_one_piece(): lax.all_to_all(both, axis, split_axis=split_dim, concat_axis=concat_dim,...  55.3 us
    reduce_scatter x1, waiting for transfers between devices, per_device(): lax.psum_scatter((jnp.dot(d_gate, gate_mat.T, preferred_element_type=jnp....  43.8 us
    all_gather x1, waiting for transfers between devices, per_device(): lax.all_gather(received[0], 'dp', axis=0, tiled=True)  19.9 us
    all_gather x1, blocking collectives, per_device(): lax.all_gather(received[2], 'dp', axis=0, tiled=True)  15.5 us
    reshape x1, local copies, waits for them, and re-layouts, per_device(): rows_x = gathered[0].reshape(-1, features)  13.1 us
    all_to_all x1, waiting for transfers between devices, per_device(): lax.all_to_all(own_rows.reshape(expert_count, capacity, features).astype(...  13.1 us
    reshape x1, local copies, waits for them, and re-layouts, per_device(): rows_dy = gathered[1].reshape(-1, features)  13 us
    all_gather x1, waiting for transfers between devices, per_device(): lax.all_gather(received[1], 'dp', axis=0, tiled=True)  11.7 us
  transfers between devices with their start and end apart: 4, of which 4 were waited for; matrix products, arithmetic and copies ran while one was open for 15% of the time, Pallas kernels for 0%

commit v1 on v0

--- a/solution.py
+++ b/solution.py
@@ -1,8 +1,39 @@
+import functools
 import math
 import jax
 import jax.numpy as jnp
 from jax import lax
 from jax.sharding import PartitionSpec as P
+
+
+def draft_ticks(mine, axis_k):
+    tall = list(mine.shape[1:])
+    tall[axis_k] *= mine.shape[0]
+    return jnp.moveaxis(mine, 0, axis_k).reshape(tall)
+
+
+def treat_face_up(values, comm_axis, axis_no):
+    q_n = lax.psum(1, comm_axis)
+    ledger = tuple(((h, (h + 1) % q_n) for h in range(q_n)))
+    crops = tuple(((nth, ix) for ix, nth in ledger))
+    after, state_next = ([], [])
+    for u in tuple(range(q_n - 1)):
+        if u % 2 == 0:
+            last = lax.ppermute(after[-1] if after else values, comm_axis, perm=ledger)
+            after.append(last)
+        else:
+            state_next.append(
+                lax.ppermute(state_next[-1] if state_next else values, comm_axis, crops)
+            )
+    r1 = jnp.stack([*after[::-1], values, *state_next])
+    everything = lax.axis_index(comm_axis)
+    seen_now = len(after)
+    piece_out = everything - seen_now
+    r1 = r1[(jnp.arange(q_n) - piece_out) % q_n]
+    return draft_ticks(r1, axis_no)
+
+
+run_views = functools.partial(treat_face_up, comm_axis="dp", axis_no=0)
 
 
 def in_one_piece(arrays, axis, split_dim, concat_dim, along):
@@ -66,7 +97,7 @@
     )
     gathered = (
         lax.all_gather(received[0], "dp", axis=0, tiled=True),
-        lax.all_gather(received[1], "dp", axis=0, tiled=True),
+        run_views(received[1]),
         lax.all_gather(received[2], "dp", axis=0, tiled=True),
     )
     rows_x = gathered[0].reshape(-1, features)

time: 288 us -> 322 us (1.12)
  local copies, waits for them, and re-layouts: 68.8 us -> 88 us
  starting transfers between devices: 9.84 us -> 23.6 us
    ppermute x0 -> x7, waiting for transfers between devices: none -> 37.3 us  [the longest x4 33.2 us: treat_face_up(): last = lax.ppermute(after[-1] if after else values, comm_axis, perm=ledger)]
    all_gather x1, waiting for transfers between devices: 19.9 us -> 0.01 us  [per_device(): lax.all_gather(received[0], 'dp', axis=0, tiled=True)]
    unnamed x28 -> x41, local copies, waits for them, and re-layouts: 1.9 us -> 17.4 us
    another operation x0 -> x2, local copies, waits for them, and re-layouts: none -> 14.5 us  [the longest x1 13 us: per_device(): rows_dy = gathered[1].reshape(-1, features)]
    ppermute x0 -> x7, starting transfers between devices: none -> 13.9 us  [the longest x4 13.7 us: treat_face_up(): last = lax.ppermute(after[-1] if after else values, comm_axis, perm=ledger)]
    reshape x1 -> x0, local copies, waits for them, and re-layouts: 13 us -> none  [per_device(): rows_dy = gathered[1].reshape(-1, features)]
    all_gather x1 -> x0, waiting for transfers between devices: 11.7 us -> none  [per_device(): lax.all_gather(received[1], 'dp', axis=0, tiled=True)]
    gather x0 -> x1, local copies, waits for them, and re-layouts: none -> 11.7 us  [treat_face_up(): r1 = r1[(jnp.arange(q_n) - piece_out) % q_n]]
  transfers between devices with their start and end apart: 4 -> 10, of which waited for: 4 -> 6; matrix products, arithmetic and copies ran while one was open for 15% -> 18% of each run, Pallas kernels for 0% -> 0%
where the time goes in v1:
time: 322 us; the launch traced here: 320 us
  waiting for transfers between devices  90.9 us (28%)
  local copies, waits for them, and re-layouts  88 us (27%)
  blocking collectives  71 us (22%)
  matrix products  26.7 us (8%)
  starting transfers between devices  23.6 us (7%)
  between operations  14.4 us (4%)
  other arithmetic  5.42 us (2%)
    all_to_all x1, blocking collectives, in_one_piece(): lax.all_to_all(both, axis, split_axis=split_dim, concat_axis=concat_dim,...  55.3 us
    reduce_scatter x1, waiting for transfers between devices, per_device(): lax.psum_scatter((jnp.dot(d_gate, gate_mat.T, preferred_element_type=jnp....  40.4 us
    ppermute x4, waiting for transfers between devices, treat_face_up(): last = lax.ppermute(after[-1] if after else values, comm_axis, perm=ledger)  33.2 us
    unnamed x41, local copies, waits for them, and re-layouts  17.4 us
    all_gather x1, blocking collectives, per_device(): lax.all_gather(received[2], 'dp', axis=0, tiled=True)  15.7 us
    ppermute x4, starting transfers between devices, treat_face_up(): last = lax.ppermute(after[-1] if after else values, comm_axis, perm=ledger)  13.7 us
    all_to_all x1, waiting for transfers between devices, per_device(): lax.all_to_all(own_rows.reshape(expert_count, capacity, features).astype(...  13.1 us
    reshape x1, local copies, waits for them, and re-layouts, per_device(): rows_x = gathered[0].reshape(-1, features)  13 us
  transfers between devices with their start and end apart: 10, of which 6 were waited for; matrix products, arithmetic and copies ran while one was open for 18% of the time, Pallas kernels for 0%

profile of v1, /device:TPU:15, one launch (start us, length us, event | category | flops | bytes accessed | tf_op | source)
XLA Modules:
  0.0 320.1 jit_solution(16097185435392169966)
XLA Ops:
  7.2 0.0 all-gather.3.cloned.1.call-start
  7.2 0.9 eq.17
  8.1 0.7 broadcast_multiply_fusion
  8.8 0.1 fusion.24
  8.9 0.1 reduce_window_sum.11
  9.0 0.2 select_reduce_fusion
  9.2 0.1 mul.58
  9.3 4.0 %scatter_custom_fusion = bf16[96,3584]{1,0:T(8,128)(2,1)S(1)} fusion(s32[64]{0:T(128)S(1)} %fusion.27, bf16[8,3584]{1,0:T(8,128)(2,1)} %param.7, s32[1024]{0:T(1024)S(1)} %pad_clamp_fusion.2, bf16[]{:T(256)} %constant.45.clone.1), kind=kCustom, calls=%fused_computation.41 | custom fusion | bytes 688640 | tf_op jit(solution)/shard_map/scatter | solution.py:84
  13.3 0.4 reshape.164
  13.7 4.0 %scatter_custom_fusion.1 = bf16[96,3584]{1,0:T(8,128)(2,1)S(1)} fusion(s32[64]{0:T(128)S(1)} %fusion.27, bf16[8,3584]{1,0:T(8,128)(2,1)} %param.8, s32[1024]{0:T(1024)S(1)} %pad_clamp_fusion.2, bf16[]{:T(256)} %constant.45.clone.1), kind=kCustom, calls=%fused_computation.39 | custom fusion | bytes 688640 | tf_op jit(solution)/shard_map/scatter | solution.py:85
  17.7 1.2 reshape.165
  18.8 0.8 reshape.227
  19.6 1.0 scatter_custom_fusion.2
  20.6 0.2 reshape_reshape.8
  20.8 1.9 pad_maximum_fusion
  22.7 55.3 %all_to_all.10 = bf16[32,3,7169]{2,1,0:T(4,128)(2,1)S(1)} all-to-all(bf16[32,3,7169]{2,1,0:T(4,128)(2,1)S(1)} %pad_maximum_fusion), channel_id=1, replica_groups=mesh['dp'=8,'expert'=32] {'expert'}, dimensions={0} | all-to-all | bytes 2752896 | tf_op jit(solution)/shard_map/all_to_all | solution.py:44
  78.0 1.3 copy-done.1
  79.3 0.6 fusion.32
  79.9 0.1 copy.15
  80.1 2.6 collective-permute-start
  82.6 7.9 %collective-permute-done = bf16[32,3,3584]{2,0,1:T(8,128)(2,1)S(1)} collective-permute-done((bf16[32,3,3584]{2,0,1:T(8,128)(2,1)S(1)}, bf16[32,3,3584]{2,0,1:T(8,128)(2,1)S(1)}, u32[]{:S(2)}, u32[]{:S(2)}) %collective-permute-start) | collective-permute-done | bytes 688160 | tf_op jit(solution)/shard_map/ppermute | solution.py:22
  90.5 3.7 %collective-permute-start.1 = (bf16[32,3,3584]{2,0,1:T(8,128)(2,1)S(1)}, bf16[32,3,3584]{2,0,1:T(8,128)(2,1)S(1)}, u32[]{:S(2)}, u32[]{:S(2)}) collective-permute-start(bf16[32,3,3584]{2,0,1:T(8,128)(2,1)S(1)} %collective-permute-done), channel_id=1, source_target_pairs={{0,32},{32,64},{64,96},{96,128},{128,160},{160,192},{192,224},{224... | collective-permute-start | bytes 2064392 | tf_op jit(solution)/shard_map/ppermute | solution.py:22
  94.2 1.0 copy.24
  95.2 0.0 all-gather.3.cloned.1.call-update
  95.2 0.0 reduce-scatter.2.cloned.1.call-start
  95.3 0.0 collective-permute-start.4
  95.3 6.8 %collective-permute-done.1 = bf16[32,3,3584]{2,0,1:T(8,128)(2,1)S(1)} collective-permute-done((bf16[32,3,3584]{2,0,1:T(8,128)(2,1)S(1)}, bf16[32,3,3584]{2,0,1:T(8,128)(2,1)S(1)}, u32[]{:S(2)}, u32[]{:S(2)}) %collective-permute-start.1) | collective-permute-done | bytes 688160 | tf_op jit(solution)/shard_map/ppermute | solution.py:22
  102.1 3.7 %collective-permute-start.2 = (bf16[32,3,3584]{2,0,1:T(8,128)(2,1)S(1)}, bf16[32,3,3584]{2,0,1:T(8,128)(2,1)}, u32[]{:S(2)}, u32[]{:S(2)}) collective-permute-start(bf16[32,3,3584]{2,0,1:T(8,128)(2,1)S(1)} %collective-permute-done.1), channel_id=1, source_target_pairs={{0,32},{32,64},{64,96},{96,128},{128,160},{160,192},{192,224},{224... | collective-permute-start | bytes 2064392 | tf_op jit(solution)/shard_map/ppermute | solution.py:22
  105.8 4.1 %collective-permute-done.4 = bf16[32,3,3584]{2,0,1:T(8,128)(2,1)} collective-permute-done((bf16[32,3,3584]{2,0,1:T(8,128)(2,1)}, bf16[32,3,3584]{2,0,1:T(8,128)(2,1)}, u32[]{:S(2)}, u32[]{:S(2)}) %collective-permute-start.4) | collective-permute-done | bytes 688160 | tf_op jit(solution)/shard_map/ppermute | solution.py:26
  109.9 18.5 %collective-permute-done.2 = bf16[32,3,3584]{2,0,1:T(8,128)(2,1)} collective-permute-done((bf16[32,3,3584]{2,0,1:T(8,128)(2,1)S(1)}, bf16[32,3,3584]{2,0,1:T(8,128)(2,1)}, u32[]{:S(2)}, u32[]{:S(2)}) %collective-permute-start.2) | collective-permute-done | bytes 688160 | tf_op jit(solution)/shard_map/ppermute | solution.py:22
  128.5 3.8 %collective-permute-start.3 = (bf16[32,3,3584]{2,0,1:T(8,128)(2,1)}, bf16[32,3,3584]{2,0,1:T(8,128)(2,1)}, u32[]{:S(2)}, u32[]{:S(2)}) collective-permute-start(bf16[32,3,3584]{2,0,1:T(8,128)(2,1)} %collective-permute-done.2), channel_id=1, source_target_pairs={{0,32},{32,64},{64,96},{96,128},{128,160},{160,192},{192,224},{224... | collective-permute-start | bytes 2064392 | tf_op jit(solution)/shard_map/ppermute | solution.py:22
  132.3 0.8 split.12
  133.1 0.3 copy.14
  133.4 15.7 %all-gather = bf16[256,3,1]{1,2,0:T(2,128)(2,1)S(1)} all-gather(bf16[32,3,1]{1,2,0:T(2,128)(2,1)S(1)} %copy.14), channel_id=2, replica_groups=mesh['dp'=8,'expert'=32] {'dp'}, dimensions={0}, use_global_device_ids=true | all-gather | bytes 1728 | tf_op jit(solution)/shard_map/all_gather | solution.py:101
  149.1 0.4 convert_reduce_fusion
  149.4 0.2 reshape.172
  149.7 0.2 collective-permute-start.6
  149.8 2.6 bitcast_dynamic-update-slice_fusion.7
  152.5 2.6 bitcast_dynamic-update-slice_fusion.6
  155.1 1.6 bitcast_dynamic-update-slice_fusion.5
  156.6 1.6 bitcast_dynamic-update-slice_fusion.4
  158.2 2.4 bitcast_dynamic-update-slice_fusion.3
  160.7 2.6 bitcast_dynamic-update-slice_fusion.2
  163.3 2.6 bitcast_dynamic-update-slice_fusion.1
  165.9 1.6 bitcast_dynamic-update-slice_fusion
  167.5 11.7 %gather_fusion = bf16[8,32,3,3584]{3,2,1,0:T(4,128)(2,1)} fusion(bf16[8,32,3,3584]{3,2,1,0:T(4,128)(2,1)} %bitcast_dynamic-update-slice_fusion, s32[1024]{0:T(1024)S(1)} %pad_clamp_fusion.1), kind=kCustom, calls=%fused_computation.2 | custom fusion | bytes 11010080 | tf_op jit(solution)/shard_map/gather | solution.py:32
  179.1 13.0 %reshape_reshape.7 = bf16[768,3584]{1,0:T(8,128)(2,1)} reshape(bf16[8,32,3,3584]{3,2,1,0:T(4,128)(2,1)} %gather_fusion) | data formatting | bytes 11010048 | tf_op jit(solution)/shard_map/reshape;reshape | solution.py:104
  192.1 10.3 %copy.25 = bf16[256,3,3584]{2,1,0:T(4,128)(2,1)} copy(bf16[256,3,3584]{2,0,1:T(8,128)(2,1)} %all-gather.3.cloned.1.call-done) | data formatting | bytes 11010048 | tf_op jit(solution)/shard_map/all_gather | solution.py:99
  202.4 13.0 %reshape.168 = bf16[768,3584]{1,0:T(8,128)(2,1)} reshape(bf16[256,3,3584]{2,1,0:T(4,128)(2,1)} %copy.25) | data formatting | bytes 11010048 | tf_op jit(solution)/shard_map/reshape | solution.py:103
  215.4 4.3 %fusion.5 = f32[768,256]{1,0:T(8,128)S(1)} fusion(bf16[768,3584]{1,0:T(8,128)(2,1)} %reshape.168, bf16[1,3584,256]{2,1,0:T(8,128)(2,1)S(1)} %copy-done), kind=kOutput, calls=%fused_computation.17 | convolution fusion | flops 1409286144 | bytes 8126464 | tf_op jit(solution)/shard_map/dot_general | solution.py:55
  219.8 3.5 %fusion.8 = f32[768,256]{1,0:T(8,128)S(1)} fusion(bf16[768,3584]{1,0:T(8,128)(2,1)S(1)} %copy-done.2, bf16[1,3584,256]{2,1,0:T(8,128)(2,1)} %param.12), kind=kOutput, calls=%fused_computation.20 | convolution fusion | flops 1409286144 | bytes 8126464 | tf_op jit(solution)/shard_map/dot_general | solution.py:56
  223.3 1.8 multiply_convert_fusion.1
  225.2 1.6 fusion.3
  226.8 4.0 %add_convert_fusion = bf16[768,3584]{1,0:T(8,128)(2,1)} fusion(f32[768,3584]{1,0:T(8,128)S(1)} %fusion.3, bf16[768,256]{1,0:T(8,128)(2,1)S(1)} %get-tuple-element.6, bf16[1,3584,256]{2,1,0:T(8,128)(2,1)S(1)} %copy-done.3), kind=kOutput, calls=%fused_computation.7 | convolution fusion | flops 1414791168 | bytes 18743296 | tf_op jit(solution)/shard_map/dot_general | solution.py:111
  230.8 40.4 %reduce-scatter.2.cloned.1.call-done = bf16[96,3584]{1,0:T(8,128)(2,1)} async-done(((bf16[768,3584]{1,0:T(8,128)(2,1)}), bf16[96,3584]{1,0:T(8,128)(2,1)}) %reduce-scatter.2.cloned.1.call-update) | async-done | bytes 688144 | tf_op jit(solution)/shard_map/reduce_scatter | solution.py:108
  271.3 2.3 convert_element_type.49
  273.5 9.6 %all-to-all-start.1 = ((bf16[32,3,3584]{2,1,0:T(4,128)(2,1)}), bf16[32,3,3584]{2,1,0:T(4,128)(2,1)}, u32[]{:S(2)}, u32[]{:S(2)}) async-start(bf16[32,3,3584]{2,1,0:T(4,128)(2,1)} %convert_element_type.49), calls=%async_computation.2 | async-start | bytes 1835008 | tf_op jit(solution)/shard_map/all_to_all | solution.py:117
  283.2 5.6 %fusion.1 = bf16[1,3584,256]{2,1,0:T(8,128)(2,1)} fusion(bf16[768,3584]{1,0:T(8,128)(2,1)} %reshape.168, bf16[768,256]{1,0:T(8,128)(2,1)} %copy-done.5), kind=kOutput, calls=%fused_computation.12 | convolution fusion | flops 1410203648 | bytes 7733248 | tf_op jit(solution)/shard_map/dot_general | solution.py:67
  288.9 2.9 fusion
  291.8 3.0 fusion.2
  294.8 13.1 %all-to-all-done.1 = bf16[32,3,3584]{2,1,0:T(4,128)(2,1)} async-done(((bf16[32,3,3584]{2,1,0:T(4,128)(2,1)}), bf16[32,3,3584]{2,1,0:T(4,128)(2,1)}, u32[]{:S(2)}, u32[]{:S(2)}) %all-to-all-start.1) | async-done | bytes 688160 | tf_op jit(solution)/shard_map/all_to_all | solution.py:117
  307.9 1.6 reshape.174
  309.5 1.8 gather_fusion.1
  311.2 2.0 bitcast_reduce_fusion
  (48 shorter events, 0.2 us)
Async XLA Ops:
  7.2 208.3 %copy-start = (bf16[1,3584,256]{2,1,0:T(8,128)(2,1)S(1)}, bf16[1,3584,256]{2,1,0:T(8,128)(2,1)}, u32[]{:S(2)}) copy-start(bf16[1,3584,256]{2,1,0:T(8,128)(2,1)} %param.11) | copy-start | bytes 5505028
  7.2 184.9 %all-gather.3.cloned.1.call-start = ((), (), s32[]{:S(2)}) async-start(), calls=%async_computation.3 | async-start | bytes 6193152 | tf_op jit(solution)/shard_map/all_gather | solution.py:99
  78.0 1.3 copy-start.1
  80.1 10.5 %copy-start.4 = (bf16[32,3,3584]{2,0,1:T(8,128)(2,1)}, bf16[32,3,3584]{2,0,1:T(8,128)(2,1)S(1)}, u32[]{:S(2)}) copy-start(bf16[32,3,3584]{2,0,1:T(8,128)(2,1)S(1)} %copy.15) | copy-start | bytes 2064388
  80.1 10.5 %collective-permute-start = (bf16[32,3,3584]{2,0,1:T(8,128)(2,1)S(1)}, bf16[32,3,3584]{2,0,1:T(8,128)(2,1)S(1)}, u32[]{:S(2)}, u32[]{:S(2)}) collective-permute-start(bf16[32,3,3584]{2,0,1:T(8,128)(2,1)S(1)} %copy.15), channel_id=1, source_target_pairs={{0,32},{32,64},{64,96},{96,128},{128,160},{160,192},{192,224},{224... | collective-permute-start | bytes 2064392 | tf_op jit(solution)/shard_map/ppermute | solution.py:22
  90.5 11.6 %collective-permute-start.1 = (bf16[32,3,3584]{2,0,1:T(8,128)(2,1)S(1)}, bf16[32,3,3584]{2,0,1:T(8,128)(2,1)S(1)}, u32[]{:S(2)}, u32[]{:S(2)}) collective-permute-start(bf16[32,3,3584]{2,0,1:T(8,128)(2,1)S(1)} %collective-permute-done), channel_id=1, source_target_pairs={{0,32},{32,64},{64,96},{96,128},{128,160},{160,192},{192,224},{224... | collective-permute-start | bytes 2064392 | tf_op jit(solution)/shard_map/ppermute | solution.py:22
  95.2 176.1 %reduce-scatter.2.cloned.1.call-start = ((), (), s32[]{:S(2)}) async-start(), calls=%async_computation.4 | async-start | bytes 6193152 | tf_op jit(solution)/shard_map/reduce_scatter | solution.py:108
  95.3 14.6 %collective-permute-start.4 = (bf16[32,3,3584]{2,0,1:T(8,128)(2,1)}, bf16[32,3,3584]{2,0,1:T(8,128)(2,1)}, u32[]{:S(2)}, u32[]{:S(2)}) collective-permute-start(bf16[32,3,3584]{2,0,1:T(8,128)(2,1)} %copy-done.4), channel_id=1, source_target_pairs={{32,0},{64,32},{96,64},{128,96},{160,128},{192,160},{224,192},{0,2... | collective-permute-start | bytes 2064392 | tf_op jit(solution)/shard_map/ppermute | solution.py:26
  102.1 26.4 %collective-permute-start.2 = (bf16[32,3,3584]{2,0,1:T(8,128)(2,1)S(1)}, bf16[32,3,3584]{2,0,1:T(8,128)(2,1)}, u32[]{:S(2)}, u32[]{:S(2)}) collective-permute-start(bf16[32,3,3584]{2,0,1:T(8,128)(2,1)S(1)} %collective-permute-done.1), channel_id=1, source_target_pairs={{0,32},{32,64},{64,96},{96,128},{128,160},{160,192},{192,224},{224... | collective-permute-start | bytes 2064392 | tf_op jit(solution)/shard_map/ppermute | solution.py:22
  109.9 39.7 %collective-permute-start.5 = (bf16[32,3,3584]{2,0,1:T(8,128)(2,1)}, bf16[32,3,3584]{2,0,1:T(8,128)(2,1)}, u32[]{:S(2)}, u32[]{:S(2)}) collective-permute-start(bf16[32,3,3584]{2,0,1:T(8,128)(2,1)} %collective-permute-done.4), channel_id=1, source_target_pairs={{32,0},{64,32},{96,64},{128,96},{160,128},{192,160},{224,192},{0,2... | collective-permute-start | bytes 2064392 | tf_op jit(solution)/shard_map/ppermute | solution.py:26
  128.5 21.4 %collective-permute-start.3 = (bf16[32,3,3584]{2,0,1:T(8,128)(2,1)}, bf16[32,3,3584]{2,0,1:T(8,128)(2,1)}, u32[]{:S(2)}, u32[]{:S(2)}) collective-permute-start(bf16[32,3,3584]{2,0,1:T(8,128)(2,1)} %collective-permute-done.2), channel_id=1, source_target_pairs={{0,32},{32,64},{64,96},{96,128},{128,160},{160,192},{192,224},{224... | collective-permute-start | bytes 2064392 | tf_op jit(solution)/shard_map/ppermute | solution.py:22
  149.7 16.2 %collective-permute-start.6 = (bf16[32,3,3584]{2,0,1:T(8,128)(2,1)}, bf16[32,3,3584]{2,0,1:T(8,128)(2,1)S(1)}, u32[]{:S(2)}, u32[]{:S(2)}) collective-permute-start(bf16[32,3,3584]{2,0,1:T(8,128)(2,1)} %collective-permute-done.5), channel_id=1, source_target_pairs={{32,0},{64,32},{96,64},{128,96},{160,128},{192,160},{224,192},{0,2... | collective-permute-start | bytes 2064392 | tf_op jit(solution)/shard_map/ppermute | solution.py:26
  215.4 4.3 %copy-start.2 = (bf16[768,3584]{1,0:T(8,128)(2,1)S(1)}, bf16[768,3584]{1,0:T(8,128)(2,1)}, u32[]{:S(2)}) copy-start(bf16[768,3584]{1,0:T(8,128)(2,1)} %reshape.168) | copy-start | bytes 16515076
  215.4 7.8 %slice-start = ((s8[5505024]{0:T(1024)(128)(4,1)}), s8[4194304]{0:T(1024)(128)(4,1)S(1)}, s32[]{:S(2)}) async-start(s8[5505024]{0:T(1024)(128)(4,1)} %bitcast.61), calls=%async_computation.5 | async-start | bytes 8388608
  219.8 5.4 %copy-start.7 = (f32[768,256]{1,0:T(8,128)}, f32[768,256]{1,0:T(8,128)S(1)}, u32[]{:S(2)}) copy-start(f32[768,256]{1,0:T(8,128)S(1)} %fusion.5) | copy-start | bytes 2359300
  219.8 3.5 %slice-start.1 = ((s8[5505024]{0:T(1024)(128)(4,1)}), s8[1310720]{0:T(1024)(128)(4,1)S(1)}, s32[]{:S(2)}) async-start(s8[5505024]{0:T(1024)(128)(4,1)} %bitcast.61), calls=%async_computation.6 | async-start | bytes 2621440
  219.8 3.5 %copy-start.6 = (bf16[1,256,3584]{2,1,0:T(8,128)(2,1)S(1)}, bf16[1,256,3584]{2,1,0:T(8,128)(2,1)}, u32[]{:S(2)}) copy-start(bf16[1,256,3584]{2,1,0:T(8,128)(2,1)} %param.13) | copy-start | bytes 5505028
  223.3 1.8 copy-start.9
  225.1 1.7 copy-start.5
  225.2 1.7 copy-start.3
  271.3 17.5 %slice-start.4 = ((s8[5505024]{0:T(1024)(128)(4,1)}), s8[1310720]{0:T(1024)(128)(4,1)S(1)}, s32[]{:S(2)}) async-start(s8[5505024]{0:T(1024)(128)(4,1)} %bitcast.65), calls=%async_computation.9 | async-start | bytes 2621440
  273.5 34.3 %all-to-all-start.1 = ((bf16[32,3,3584]{2,1,0:T(4,128)(2,1)}), bf16[32,3,3584]{2,1,0:T(4,128)(2,1)}, u32[]{:S(2)}, u32[]{:S(2)}) async-start(bf16[32,3,3584]{2,1,0:T(4,128)(2,1)} %convert_element_type.49), calls=%async_computation.2 | async-start | bytes 1835008 | tf_op jit(solution)/shard_map/all_to_all | solution.py:117
  283.2 5.7 %slice-start.5 = ((s8[5505024]{0:T(1024)(128)(4,1)}), s8[4194304]{0:T(1024)(128)(4,1)S(1)}, s32[]{:S(2)}) async-start(s8[5505024]{0:T(1024)(128)(4,1)} %bitcast.65), calls=%async_computation.10 | async-start | bytes 8388608
  283.2 8.6 %slice-start.2 = ((s8[5505024]{0:T(1024)(128)(4,1)}), s8[4194304]{0:T(1024)(128)(4,1)S(1)}, s32[]{:S(2)}) async-start(s8[5505024]{0:T(1024)(128)(4,1)} %bitcast.63), calls=%async_computation.7 | async-start | bytes 8388608
  288.8 2.9 slice-start.3
  288.8 2.9 copy-start.8
  288.9 2.9 copy-start.10
Sparse Core Ops, SparseCore 0:
  95.3 44.0 all-gather.2
  231.0 40.2 reduce-scatter.1
